TPU v7x, 32 devices: a whole 2x2x4 slice. The times are simulated.
32 devices in a mesh: blk: 8 (over z, y), pix: 4 (over x, core).
Axes of the slice: x: 2, y: 2, z: 4, core: 2. Of those that a mesh axis runs over, the one named last changes fastest.
Arguments:
- images: bfloat16 [256, 16384], P('blk', 'pix'), may hold values from -14 to 14
- templates: bfloat16 [2304, 16384], P('blk', 'pix'), may hold values from -4 to 4
- routes: int32 [256, 4], P('blk'), may hold values from 0 to 7, all different within a row; in each aligned block of 32 rows (0 to 31, 32 to 63, ...) at most 24 rows name the same one
- image_weight: float32 [256], P('blk'), may hold values from 0.25 to 4
- template_weight: float32 [2304], P('blk'), may hold values from 0.25 to 4
Outputs:
- template_means: bfloat16 [2304, 16384], P('blk', 'pix')
- image_duals: float32 [256], P('blk')
Inputs may be any that keep to these rules, and one draw needn't show every extreme that they name: `routes`: each image names 4 different template blocks. Among the 32 images of one block, at most 24 name any one template block, and some template block is named by exactly 24 of them. Every template block is named by some image.
All inputs are finite; a program needn't handle non-finite values.
Results may differ from a plain program's by a relative error of at most 0.0046.
Values may be sent and summed in bfloat16 or wider, within the bound.
A program may use at most 64 MiB of HBM per device.

v0:
```python
import jax
import jax.numpy as jnp
from jax import lax
from jax.sharding import PartitionSpec as P

SWEEPS = 2


def on_device(images, templates, routes, image_weight, template_weight):
    blocks = lax.axis_size("blk")
    img_dev = images.shape[0]
    admits = routes.shape[1]
    capacity = max(2, (3 * img_dev * admits + 2 * blocks - 1) // (2 * blocks))
    target = routes.reshape(-1)
    target_hot = (target[:, None] == jnp.arange(blocks, dtype=jnp.int32)[None, :]).astype(jnp.int32)
    before = jnp.cumsum(target_hot, axis=0) - target_hot
    position = jnp.sum(before * target_hot, axis=1)
    slot_of = target * capacity + position
    wanted = jnp.arange(blocks * capacity, dtype=jnp.int32)
    matches = slot_of[None, :] == wanted[:, None]
    filled = jnp.any(matches, axis=1)
    owner_image = jnp.sum(
        jnp.where(matches, jnp.arange(target.shape[0], dtype=jnp.int32)[None, :] // admits, 0),
        axis=1,
    )
    outgoing = jnp.where(filled[:, None], images[owner_image], jnp.zeros((), images.dtype))
    outgoing = outgoing.reshape(blocks, capacity, images.shape[1])
    slot_flags = filled.astype(jnp.bfloat16).reshape(blocks, capacity)
    template_log = jnp.log(template_weight)
    arrived_piece = lax.all_to_all(outgoing, "blk", split_axis=0, concat_axis=0, tiled=True)
    marks_piece = lax.all_to_all(slot_flags, "blk", split_axis=0, concat_axis=0, tiled=True)
    partial_value = jnp.einsum(
        "bmp,tp->bmt", arrived_piece, templates, preferred_element_type=jnp.float32
    )
    summed = lax.psum(partial_value, "pix")
    usable = marks_piece > 0
    image_log = jnp.log(image_weight)
    slot_duals = jnp.zeros((blocks, capacity), jnp.float32)
    image_duals = jnp.zeros((img_dev,), jnp.float32)
    for sweep_index in range(SWEEPS):
        column_terms = jnp.where(usable[:, :, None], summed + slot_duals[:, :, None], -jnp.inf)
        column_peak = jnp.max(column_terms, axis=(0, 1))
        template_duals = (
            template_log
            - column_peak
            - jnp.log(jnp.sum(jnp.exp(column_terms - column_peak), axis=(0, 1)))
        )
        row_terms = summed + template_duals
        row_peak = jnp.max(row_terms, axis=2)
        row_total = jnp.sum(jnp.exp(row_terms - row_peak[:, :, None]), axis=2)
        levels = row_peak + jnp.log(row_total)
        back_levels = lax.all_to_all(levels, "blk", split_axis=0, concat_axis=0, tiled=True)
        level_routes = back_levels.reshape(-1)[slot_of].reshape(img_dev, admits)
        route_peak = jnp.max(level_routes, axis=1)
        image_duals = (
            image_log
            - route_peak
            - jnp.log(jnp.sum(jnp.exp(level_routes - route_peak[:, None]), axis=1))
        )
        duals_send = jnp.where(filled, image_duals[owner_image], 0.0).reshape(blocks, capacity)
        slot_duals = lax.all_to_all(duals_send, "blk", split_axis=0, concat_axis=0, tiled=True)
    column_terms = jnp.where(usable[:, :, None], summed + slot_duals[:, :, None], -jnp.inf)
    column_peak = jnp.max(column_terms, axis=(0, 1))
    column_exp = jnp.exp(column_terms - column_peak)
    plan_weights = (column_exp / jnp.sum(column_exp, axis=(0, 1))).astype(jnp.bfloat16)
    template_means = jnp.einsum(
        "bmt,bmp->tp", plan_weights, arrived_piece, preferred_element_type=jnp.float32
    ).astype(jnp.bfloat16)
    return (template_means, image_duals)


def solution(mesh):
    in_specs = (P("blk", "pix"), P("blk", "pix"), P("blk", None), P("blk"), P("blk"))
    out_specs = (P("blk", "pix"), P("blk"))
    return jax.shard_map(
        on_device, mesh=mesh, in_specs=in_specs, out_specs=out_specs, check_vma=False
    )
```

profile of v0, /device:TPU:0, one launch (start us, length us, event | category | flops | bytes accessed | tf_op | source)
XLA Modules:
  0.0 203.8 jit_solution(13468316568536961378)
XLA Ops:
  7.2 0.9 copy.17
  9.0 2.7 %gather_fusion = bf16[192,4096]{1,0:T(8,128)(2,1)} fusion(bf16[32,4096]{1,0:T(8,128)(2,1)S(1)} %copy-done.1, s32[1024]{0:T(1024)S(1)} %pad_clamp_fusion.1), kind=kCustom, calls=%fused_computation | custom fusion | bytes 3146496 | tf_op jit(solution)/shard_map/gather | solution.py:26
  11.7 2.7 %broadcast_select_fusion = bf16[8,24,4096]{2,1,0:T(8,128)(2,1)} fusion(bf16[8,24,4096]{2,1,0:T(8,128)(2,1)} %bitcast.88, pred[8,24]{1,0:T(8,128)(4,1)S(1)} %broadcast_in_dim.77), kind=kLoop, calls=%fused_computation.7 | loop fusion | flops 786432 | bytes 3145920 | tf_op jit(solution)/shard_map/jit(_where)/select_n | solution.py:26
  14.4 7.4 %all-to-all-start.1 = ((bf16[8,24,4096]{2,1,0:T(8,128)(2,1)}), bf16[8,24,4096]{2,1,0:T(8,128)(2,1)}, u32[]{:S(2)}, u32[]{:S(2)}) async-start(bf16[8,24,4096]{2,1,0:T(8,128)(2,1)} %broadcast_select_fusion), calls=%async_computation.1 | async-start | bytes 3145728 | tf_op jit(solution)/shard_map/all_to_all | solution.py:30
  22.1 0.7 reshape.347
  22.8 36.2 %all-to-all-done.1 = bf16[8,24,4096]{2,1,0:T(8,128)(2,1)} async-done(((bf16[8,24,4096]{2,1,0:T(8,128)(2,1)}), bf16[8,24,4096]{2,1,0:T(8,128)(2,1)}, u32[]{:S(2)}, u32[]{:S(2)}) %all-to-all-start.1) | async-done | bytes 1572896 | tf_op jit(solution)/shard_map/all_to_all | solution.py:30
  59.0 3.6 %all-to-all-start = ((bf16[8,1,24]{2,1,0:T(2,128)(2,1)}), bf16[8,1,24]{2,1,0:T(2,128)(2,1)S(1)}, u32[]{:S(2)}, u32[]{:S(2)}) async-start(bf16[8,1,24]{2,1,0:T(2,128)(2,1)} %reshape.347), calls=%async_computation | async-start | bytes 8192 | tf_op jit(solution)/shard_map/all_to_all | solution.py:31
  62.7 3.3 %fusion.1 = f32[8,24,288]{2,1,0:T(8,128)} fusion(bf16[8,24,4096]{2,1,0:T(8,128)(2,1)} %all-to-all-done.1, bf16[288,4096]{1,0:T(8,128)(2,1)S(1)} %copy-done), kind=kOutput, calls=%fused_computation.5 | convolution fusion | flops 452984832 | bytes 4153344 | tf_op jit(solution)/shard_map/bmp,tp->bmt/dot_general | solution.py:32
  66.0 3.1 %all-to-all-done = bf16[8,1,24]{2,1,0:T(2,128)(2,1)S(1)} async-done(((bf16[8,1,24]{2,1,0:T(2,128)(2,1)}), bf16[8,1,24]{2,1,0:T(2,128)(2,1)S(1)}, u32[]{:S(2)}, u32[]{:S(2)}) %all-to-all-start) | async-done | bytes 416 | tf_op jit(solution)/shard_map/all_to_all | solution.py:31
  69.1 31.1 %all-reduce.2.cloned.1.call-done = f32[8,24,288]{2,1,0:T(8,128)} async-done(((f32[8,24,288]{2,1,0:T(8,128)}), f32[8,24,288]{2,1,0:T(8,128)}) %all-reduce.2.cloned.1.call-update) | async-done | bytes 221200 | tf_op jit(solution)/shard_map/psum | solution.py:35
  100.2 1.1 select_reduce_fusion
  101.3 1.1 exponential_reduce_fusion.3
  102.5 1.1 add_reduce_fusion.1
  103.5 1.2 exponential_reduce_fusion.2
  104.7 0.6 log_add_fusion.1
  105.3 5.5 %all-to-all-start.2 = ((f32[8,1,24]{2,1,0:T(1,128)}), f32[8,1,24]{2,1,0:T(1,128)S(1)}, u32[]{:S(2)}, u32[]{:S(2)}) async-start(f32[8,1,24]{2,1,0:T(1,128)} %bitcast.5), calls=%async_computation.2 | async-start | bytes 8192 | tf_op jit(solution)/shard_map/all_to_all | solution.py:52
  110.8 6.4 %all-to-all-done.2 = f32[8,1,24]{2,1,0:T(1,128)S(1)} async-done(((f32[8,1,24]{2,1,0:T(1,128)}), f32[8,1,24]{2,1,0:T(1,128)S(1)}, u32[]{:S(2)}, u32[]{:S(2)}) %all-to-all-start.2) | async-done | bytes 800 | tf_op jit(solution)/shard_map/all_to_all | solution.py:52
  117.2 0.5 broadcast.505
  117.7 0.7 reduce.6
  118.5 1.3 gather_fusion.1
  120.2 0.7 fusion.18
  120.9 0.7 fusion.17
  121.6 19.9 %select_select_fusion.1 = f32[192]{0:T(256)S(1)} fusion(pred[192]{0:T(512)(128)(4,1)S(1)} %fusion.11, f32[]{:T(128)} %bitcast.8, f32[]{:T(128)} %bitcast.9, f32[]{:T(128)} %bitcast.10, f32[]{:T(128)} %bitcast.11, f32[]{:T(128)} %bitcast.12, f32[]{:T(128)} %bitcast.13, f32[]{:T(128)} %bitcast.14, f32[]{:T(128)} %bitcast.15, f32[]{:T(128)} %bitcast.16, ...), kind=kLoop, calls=%fused_computation.46 | loop fusion | flops 12096 | bytes 1856 | tf_op jit(solution)/shard_map/jit(_where)/select_n | solution.py:60
  141.6 8.8 %all_to_all.35 = f32[8,1,24]{2,1,0:T(1,128)S(1)} all-to-all(f32[8,1,24]{2,1,0:T(1,128)S(1)} %select_n.88), channel_id=1, replica_groups=mesh['blk'=8,'pix'=4] {'blk'}, dimensions={0} | all-to-all | bytes 1536 | tf_op jit(solution)/shard_map/all_to_all | solution.py:61
  151.1 8.9 %all_to_all.36 = f32[8,1,24]{2,1,0:T(1,128)S(1)} all-to-all(f32[8,1,24]{2,1,0:T(1,128)S(1)} %bitcast.97), channel_id=1, replica_groups=mesh['blk'=8,'pix'=4] {'blk'}, dimensions={0} | all-to-all | bytes 1536 | tf_op jit(solution)/shard_map/all_to_all | solution.py:52
  159.9 0.7 reduce.7
  160.7 1.3 gather_fusion.2
  162.4 0.7 fusion.16
  163.1 0.7 fusion.15
  163.8 20.1 %select_select_fusion = f32[192]{0:T(256)S(1)} fusion(pred[192]{0:T(512)(128)(4,1)S(1)} %fusion.11, f32[]{:T(128)} %bitcast.42, f32[]{:T(128)} %bitcast.43, f32[]{:T(128)} %bitcast.44, f32[]{:T(128)} %bitcast.45, f32[]{:T(128)} %bitcast.46, f32[]{:T(128)} %bitcast.47, f32[]{:T(128)} %bitcast.48, f32[]{:T(128)} %bitcast.49, f32[]{:T(128)} %bitcast.50, ...), kind=kLoop, calls=%fused_computation.45 | loop fusion | flops 12096 | bytes 1856 | tf_op jit(solution)/shard_map/jit(_where)/select_n | solution.py:60
  184.0 8.8 %all_to_all.37 = f32[8,1,24]{2,1,0:T(1,128)S(1)} all-to-all(f32[8,1,24]{2,1,0:T(1,128)S(1)} %select_n.91), channel_id=1, replica_groups=mesh['blk'=8,'pix'=4] {'blk'}, dimensions={0} | all-to-all | bytes 1536 | tf_op jit(solution)/shard_map/all_to_all | solution.py:61
  193.2 3.7 %fusion = bf16[288,4096]{1,0:T(8,128)(2,1)} fusion(bf16[8,24,4096]{2,1,0:T(8,128)(2,1)} %all-to-all-done.1, f32[8,24,288]{2,1,0:T(8,128)S(1)} %copy-done.2, f32[288]{0:T(512)S(1)} %fusion.5, f32[288]{0:T(512)S(1)} %fusion.4, f32[8,24]{1,0:T(8,128)S(1)} %bitcast.91, pred[8,24]{1,0:T(8,128)(4,1)S(1)} %compare_bitcast_fusion), kind=kOutput, calls=%fused_computation.4 | convolution fusion | flops 454440960 | bytes 4156608 | tf_op jit(solution)/shard_map/bmt,bmp->tp/dot_general | solution.py:66
  (54 shorter events, 3.2 us)
Async XLA Ops:
  7.2 55.5 %copy-start = (bf16[288,4096]{1,0:T(8,128)(2,1)S(1)}, bf16[288,4096]{1,0:T(8,128)(2,1)}, u32[]{:S(2)}) copy-start(bf16[288,4096]{1,0:T(8,128)(2,1)} %param.6) | copy-start | bytes 7077892
  7.2 1.8 copy-start.1
  14.4 7.5 %copy-start.4 = (s32[32,4]{0,1:T(4,128)S(1)}, s32[32,4]{0,1:T(4,128)}, u32[]{:S(2)}) copy-start(s32[32,4]{0,1:T(4,128)} %param.7) | copy-start | bytes 1540
  14.4 44.5 %all-to-all-start.1 = ((bf16[8,24,4096]{2,1,0:T(8,128)(2,1)}), bf16[8,24,4096]{2,1,0:T(8,128)(2,1)}, u32[]{:S(2)}, u32[]{:S(2)}) async-start(bf16[8,24,4096]{2,1,0:T(8,128)(2,1)} %broadcast_select_fusion), calls=%async_computation.1 | async-start | bytes 3145728 | tf_op jit(solution)/shard_map/all_to_all | solution.py:30
  59.0 10.1 %all-to-all-start = ((bf16[8,1,24]{2,1,0:T(2,128)(2,1)}), bf16[8,1,24]{2,1,0:T(2,128)(2,1)S(1)}, u32[]{:S(2)}, u32[]{:S(2)}) async-start(bf16[8,1,24]{2,1,0:T(2,128)(2,1)} %reshape.347), calls=%async_computation | async-start | bytes 8192 | tf_op jit(solution)/shard_map/all_to_all | solution.py:31
  62.6 39.8 %copy-start.5 = (f32[288]{0:T(512)S(1)}, f32[288]{0:T(512)}, u32[]{:S(2)}) copy-start(f32[288]{0:T(512)} %param.9) | copy-start | bytes 3460
  62.6 37.6 %all-reduce.2.cloned.1.call-start = ((), (), s32[]{:S(2)}) async-start(), calls=%async_computation.6 | async-start | bytes 589824 | tf_op jit(solution)/shard_map/psum | solution.py:35
  66.0 54.2 %copy-start.6 = (f32[32]{0:T(128)S(1)}, f32[32]{0:T(128)}, u32[]{:S(2)}) copy-start(f32[32]{0:T(128)} %param.8) | copy-start | bytes 388
  100.2 50.3 %copy-start.2 = (f32[8,24,288]{2,1,0:T(8,128)S(1)}, f32[8,24,288]{2,1,0:T(8,128)}, u32[]{:S(2)}) copy-start(f32[8,24,288]{2,1,0:T(8,128)} %all-reduce.2.cloned.1.call-done) | copy-start | bytes 663556
  105.3 11.9 %all-to-all-start.2 = ((f32[8,1,24]{2,1,0:T(1,128)}), f32[8,1,24]{2,1,0:T(1,128)S(1)}, u32[]{:S(2)}, u32[]{:S(2)}) async-start(f32[8,1,24]{2,1,0:T(1,128)} %bitcast.5), calls=%async_computation.2 | async-start | bytes 8192 | tf_op jit(solution)/shard_map/all_to_all | solution.py:52
  162.4 34.5 %copy-start.3 = (f32[32]{0:T(128)}, f32[32]{0:T(128)S(1)}, u32[]{:S(2)}) copy-start(f32[32]{0:T(128)S(1)} %log_subtract_fusion.2) | copy-start | bytes 388
Sparse Core Ops, SparseCore 0:
  66.3 33.7 all-reduce.1
where the time goes:
time: 205 us; the launch traced here: 204 us
  waiting for transfers between devices  76.8 us (37%)
  other arithmetic  51.3 us (25%)
  blocking collectives  26.6 us (13%)
  starting transfers between devices  16.6 us (8%)
  between operations  14.3 us (7%)
  local copies, waits for them, and re-layouts  11.1 us (5%)
  matrix products  7.05 us (3%)
    select_n x2, other arithmetic, on_device(): jnp.where(filled, image_duals[owner_image], 0.0).reshape(blocks, capacity)  40 us
    all_to_all x1, waiting for transfers between devices, on_device(): lax.all_to_all(outgoing, 'blk', split_axis=0, concat_axis=0, tiled=True)  36.2 us
    psum x1, waiting for transfers between devices, on_device(): summed = lax.psum(partial_value, 'pix')  31.1 us
    all_to_all x2, blocking collectives, on_device(): lax.all_to_all(duals_send, 'blk', split_axis=0, concat_axis=0, tiled=True)  17.7 us
    all_to_all x1, blocking collectives, on_device(): lax.all_to_all(levels, 'blk', split_axis=0, concat_axis=0, tiled=True)  8.86 us
    all_to_all x1, starting transfers between devices, on_device(): lax.all_to_all(outgoing, 'blk', split_axis=0, concat_axis=0, tiled=True)  7.44 us
    all_to_all x1, waiting for transfers between devices, on_device(): lax.all_to_all(levels, 'blk', split_axis=0, concat_axis=0, tiled=True)  6.41 us
    all_to_all x1, starting transfers between devices, on_device(): lax.all_to_all(levels, 'blk', split_axis=0, concat_axis=0, tiled=True)  5.52 us
  transfers between devices with their start and end apart: 4, of which 4 were waited for; matrix products, arithmetic and copies ran while one was open for 2% of the time, Pallas kernels for 0%

commit v1 on v0

--- a/solution.py
+++ b/solution.py
@@ -4,6 +4,22 @@
 from jax.sharding import PartitionSpec as P
 
 SWEEPS = 2
+
+
+def pass_knots(q_in, dimension_no, here_x):
+    small = q_in.shape
+    prior = q_in.reshape(
+        *small[:dimension_no], here_x, small[dimension_no] // here_x, *small[dimension_no + 1 :]
+    )
+    block_out = jnp.moveaxis(prior, dimension_no, 0)
+    return block_out
+
+
+def produce_results(obj, which_dim):
+    z_new = list(obj.shape[1:])
+    z_new[which_dim] *= obj.shape[0]
+    opened = jnp.moveaxis(obj, 0, which_dim).reshape(z_new)
+    return opened
 
 
 def on_device(images, templates, routes, image_weight, template_weight):
@@ -49,7 +65,22 @@
         row_peak = jnp.max(row_terms, axis=2)
         row_total = jnp.sum(jnp.exp(row_terms - row_peak[:, :, None]), axis=2)
         levels = row_peak + jnp.log(row_total)
-        back_levels = lax.all_to_all(levels, "blk", split_axis=0, concat_axis=0, tiled=True)
+        w_next = jax.lax.psum(1, axis_name="blk")
+        finding = jax.lax.axis_index("blk")
+        carry_out, shaped = (w_next, finding)
+        r2 = pass_knots(levels, 0, carry_out)
+        so_far_all = [r2[shaped]]
+        for i in range(1, carry_out):
+            tile_out = r2[(shaped + i) % carry_out]
+            t1 = jax.lax.ppermute(
+                tile_out,
+                axis_name="blk",
+                perm=[(rr, (rr + i) % carry_out) for rr in range(carry_out)],
+            )
+            so_far_all.append(t1)
+        new = jnp.stack(so_far_all, axis=0)
+        r2 = new[(shaped - jnp.arange(carry_out)) % carry_out]
+        back_levels = produce_results(r2, 0)
         level_routes = back_levels.reshape(-1)[slot_of].reshape(img_dev, admits)
         route_peak = jnp.max(level_routes, axis=1)
         image_duals = (

time: 205 us -> 213 us (1.039)
  starting transfers between devices: 16.6 us -> 30.3 us
  blocking collectives: 26.6 us -> 17.9 us
  waiting for transfers between devices: 76.8 us -> 81.4 us
    ppermute x0 -> x14, starting transfers between devices: none -> 19.2 us  [on_device(): jax.lax.ppermute(tile_out, axis_name='blk', perm=[(rr, (rr + i) % carry_o...]
    ppermute x0 -> x14, waiting for transfers between devices: none -> 11 us  [on_device(): jax.lax.ppermute(tile_out, axis_name='blk', perm=[(rr, (rr + i) % carry_o...]
    all_to_all x1 -> x0, blocking collectives: 8.86 us -> none  [on_device(): lax.all_to_all(levels, 'blk', split_axis=0, concat_axis=0, tiled=True)]
    all_to_all x1 -> x0, waiting for transfers between devices: 6.41 us -> none  [on_device(): lax.all_to_all(levels, 'blk', split_axis=0, concat_axis=0, tiled=True)]
    all_to_all x1 -> x0, starting transfers between devices: 5.52 us -> none  [on_device(): lax.all_to_all(levels, 'blk', split_axis=0, concat_axis=0, tiled=True)]
  transfers between devices with their start and end apart: 4 -> 17, of which waited for: 4 -> 9; matrix products, arithmetic and copies ran while one was open for 2% -> 2% of each run, Pallas kernels for 0% -> 0%
where the time goes in v1:
time: 213 us; the launch traced here: 212 us
  waiting for transfers between devices  81.4 us (38%)
  other arithmetic  49.5 us (23%)
  starting transfers between devices  30.3 us (14%)
  blocking collectives  17.9 us (8%)
  between operations  14.4 us (7%)
  local copies, waits for them, and re-layouts  11.8 us (6%)
  matrix products  7.05 us (3%)
    select_n x2, other arithmetic, on_device(): jnp.where(filled, image_duals[owner_image], 0.0).reshape(blocks, capacity)  40.1 us
    all_to_all x1, waiting for transfers between devices, on_device(): lax.all_to_all(outgoing, 'blk', split_axis=0, concat_axis=0, tiled=True)  36.1 us
    psum x1, waiting for transfers between devices, on_device(): summed = lax.psum(partial_value, 'pix')  31.1 us
    ppermute x14, starting transfers between devices, on_device(): jax.lax.ppermute(tile_out, axis_name='blk', perm=[(rr, (rr + i) % carry_o...  19.2 us
    all_to_all x2, blocking collectives, on_device(): lax.all_to_all(duals_send, 'blk', split_axis=0, concat_axis=0, tiled=True)  17.9 us
    ppermute x14, waiting for transfers between devices, on_device(): jax.lax.ppermute(tile_out, axis_name='blk', perm=[(rr, (rr + i) % carry_o...  11 us
    all_to_all x1, starting transfers between devices, on_device(): lax.all_to_all(outgoing, 'blk', split_axis=0, concat_axis=0, tiled=True)  7.44 us
  transfers between devices with their start and end apart: 17, of which 9 were waited for; matrix products, arithmetic and copies ran while one was open for 2% of the time, Pallas kernels for 0%

profile of v1, /device:TPU:0, one launch (start us, length us, event | category | flops | bytes accessed | tf_op | source)
XLA Modules:
  0.0 212.3 jit_solution(5009476633730164910)
XLA Ops:
  9.0 2.7 %gather_fusion = bf16[192,4096]{1,0:T(8,128)(2,1)} fusion(bf16[32,4096]{1,0:T(8,128)(2,1)S(1)} %copy-done.1, s32[1024]{0:T(1024)S(1)} %pad_clamp_fusion.2), kind=kCustom, calls=%fused_computation | custom fusion | bytes 3146496 | tf_op jit(solution)/shard_map/gather | solution.py:42
  11.7 2.7 %broadcast_select_fusion = bf16[8,24,4096]{2,1,0:T(8,128)(2,1)} fusion(bf16[8,24,4096]{2,1,0:T(8,128)(2,1)} %bitcast.140, pred[8,24]{1,0:T(8,128)(4,1)S(1)} %broadcast_in_dim.52), kind=kLoop, calls=%fused_computation.9 | loop fusion | flops 786432 | bytes 3145920 | tf_op jit(solution)/shard_map/jit(_where)/select_n | solution.py:42
  14.4 7.4 %all-to-all-start.1 = ((bf16[8,24,4096]{2,1,0:T(8,128)(2,1)}), bf16[8,24,4096]{2,1,0:T(8,128)(2,1)}, u32[]{:S(2)}, u32[]{:S(2)}) async-start(bf16[8,24,4096]{2,1,0:T(8,128)(2,1)} %broadcast_select_fusion), calls=%async_computation.1 | async-start | bytes 3145728 | tf_op jit(solution)/shard_map/all_to_all | solution.py:46
  22.8 36.1 %all-to-all-done.1 = bf16[8,24,4096]{2,1,0:T(8,128)(2,1)} async-done(((bf16[8,24,4096]{2,1,0:T(8,128)(2,1)}), bf16[8,24,4096]{2,1,0:T(8,128)(2,1)}, u32[]{:S(2)}, u32[]{:S(2)}) %all-to-all-start.1) | async-done | bytes 1572896 | tf_op jit(solution)/shard_map/all_to_all | solution.py:46
  59.0 3.6 %all-to-all-start = ((bf16[8,1,24]{2,1,0:T(2,128)(2,1)}), bf16[8,1,24]{2,1,0:T(2,128)(2,1)S(1)}, u32[]{:S(2)}, u32[]{:S(2)}) async-start(bf16[8,1,24]{2,1,0:T(2,128)(2,1)} %reshape.404), calls=%async_computation | async-start | bytes 8192 | tf_op jit(solution)/shard_map/all_to_all | solution.py:47
  62.7 3.3 %fusion.1 = f32[8,24,288]{2,1,0:T(8,128)} fusion(bf16[8,24,4096]{2,1,0:T(8,128)(2,1)} %all-to-all-done.1, bf16[288,4096]{1,0:T(8,128)(2,1)S(1)} %copy-done), kind=kOutput, calls=%fused_computation.7 | convolution fusion | flops 452984832 | bytes 4153344 | tf_op jit(solution)/shard_map/bmp,tp->bmt/dot_general | solution.py:48
  66.0 3.1 %all-to-all-done = bf16[8,1,24]{2,1,0:T(2,128)(2,1)S(1)} async-done(((bf16[8,1,24]{2,1,0:T(2,128)(2,1)}), bf16[8,1,24]{2,1,0:T(2,128)(2,1)S(1)}, u32[]{:S(2)}, u32[]{:S(2)}) %all-to-all-start) | async-done | bytes 416 | tf_op jit(solution)/shard_map/all_to_all | solution.py:47
  69.1 31.1 %all-reduce.2.cloned.1.call-done = f32[8,24,288]{2,1,0:T(8,128)} async-done(((f32[8,24,288]{2,1,0:T(8,128)}), f32[8,24,288]{2,1,0:T(8,128)}) %all-reduce.2.cloned.1.call-update) | async-done | bytes 221200 | tf_op jit(solution)/shard_map/psum | solution.py:51
  100.2 1.1 select_reduce_fusion
  101.3 1.1 exponential_reduce_fusion.3
  102.5 1.1 add_reduce_fusion.1
  103.5 1.2 exponential_reduce_fusion.2
  104.7 4.3 %collective-permute-start.6 = (f32[1,24]{1,0:T(1,128)S(1)}, f32[1,24]{1,0:T(1,128)S(1)}, u32[]{:S(2)}, u32[]{:S(2)}) collective-permute-start(f32[1,24]{1,0:T(1,128)S(1)} %get-tuple-element.10), channel_id=1, source_target_pairs={{0,28},{4,0},{8,4},{12,8},{16,12},{20,16},{24,20},{28,24},{1,29},{... | collective-permute-start | bytes 296 | tf_op jit(solution)/shard_map/ppermute | solution.py:75
  109.6 2.9 %collective-permute-start.3 = (f32[1,24]{1,0:T(1,128)S(1)}, f32[1,24]{1,0:T(1,128)S(1)}, u32[]{:S(2)}, u32[]{:S(2)}) collective-permute-start(f32[1,24]{1,0:T(1,128)S(1)} %get-tuple-element.13), channel_id=1, source_target_pairs={{0,16},{4,20},{8,24},{12,28},{16,0},{20,4},{24,8},{28,12},{1,17},{... | collective-permute-start | bytes 296 | tf_op jit(solution)/shard_map/ppermute | solution.py:75
  112.5 2.0 collective-permute-start.1
  115.5 2.4 %collective-permute-done.2 = f32[1,24]{1,0:T(1,128)S(1)} collective-permute-done((f32[1,24]{1,0:T(1,128)S(1)}, f32[1,24]{1,0:T(1,128)S(1)}, u32[]{:S(2)}, u32[]{:S(2)}) %collective-permute-start.2) | collective-permute-done | bytes 128 | tf_op jit(solution)/shard_map/ppermute | solution.py:75
  118.8 2.0 collective-permute-done
  121.4 1.3 gather_fusion.2
  124.6 20.0 %select_select_fusion.1 = f32[192]{0:T(256)S(1)} fusion(pred[192]{0:T(512)(128)(4,1)S(1)} %fusion.11, f32[]{:T(128)} %bitcast.25, f32[]{:T(128)} %bitcast.26, f32[]{:T(128)} %bitcast.27, f32[]{:T(128)} %bitcast.28, f32[]{:T(128)} %bitcast.29, f32[]{:T(128)} %bitcast.30, f32[]{:T(128)} %bitcast.31, f32[]{:T(128)} %bitcast.32, f32[]{:T(128)} %bitcast.33, ...), kind=kLoop, calls=%fused_computation.69 | loop fusion | flops 12096 | bytes 1856 | tf_op jit(solution)/shard_map/jit(_where)/select_n | solution.py:91
  144.6 9.1 %all_to_all.23 = f32[8,1,24]{2,1,0:T(1,128)S(1)} all-to-all(f32[8,1,24]{2,1,0:T(1,128)S(1)} %select_n.208), channel_id=1, replica_groups=mesh['blk'=8,'pix'=4] {'blk'}, dimensions={0} | all-to-all | bytes 1536 | tf_op jit(solution)/shard_map/all_to_all | solution.py:92
  155.0 1.4 collective-permute-start.12
  156.4 1.5 collective-permute-start.11
  157.9 1.5 collective-permute-start.10
  159.4 1.5 collective-permute-start.9
  160.8 1.5 collective-permute-start.8
  162.9 1.9 collective-permute-done.9
  164.7 1.5 collective-permute-done.8
  166.2 2.4 %collective-permute-done.7 = f32[1,24]{1,0:T(1,128)S(1)} collective-permute-done((f32[1,24]{1,0:T(1,128)S(1)}, f32[1,24]{1,0:T(1,128)S(1)}, u32[]{:S(2)}, u32[]{:S(2)}) %collective-permute-start.7) | collective-permute-done | bytes 128 | tf_op jit(solution)/shard_map/ppermute | solution.py:75
  169.2 1.3 gather_fusion.4
  172.4 20.1 %select_select_fusion = f32[192]{0:T(256)S(1)} fusion(pred[192]{0:T(512)(128)(4,1)S(1)} %fusion.11, f32[]{:T(128)} %bitcast.75, f32[]{:T(128)} %bitcast.76, f32[]{:T(128)} %bitcast.77, f32[]{:T(128)} %bitcast.78, f32[]{:T(128)} %bitcast.79, f32[]{:T(128)} %bitcast.80, f32[]{:T(128)} %bitcast.81, f32[]{:T(128)} %bitcast.82, f32[]{:T(128)} %bitcast.83, ...), kind=kLoop, calls=%fused_computation.68 | loop fusion | flops 12096 | bytes 1856 | tf_op jit(solution)/shard_map/jit(_where)/select_n | solution.py:91
  192.6 8.8 %all_to_all.24 = f32[8,1,24]{2,1,0:T(1,128)S(1)} all-to-all(f32[8,1,24]{2,1,0:T(1,128)S(1)} %select_n.211), channel_id=1, replica_groups=mesh['blk'=8,'pix'=4] {'blk'}, dimensions={0} | all-to-all | bytes 1536 | tf_op jit(solution)/shard_map/all_to_all | solution.py:92
  201.7 3.7 %fusion = bf16[288,4096]{1,0:T(8,128)(2,1)} fusion(bf16[8,24,4096]{2,1,0:T(8,128)(2,1)} %all-to-all-done.1, f32[8,24,288]{2,1,0:T(8,128)S(1)} %copy-done.2, f32[288]{0:T(512)S(1)} %fusion.5, f32[288]{0:T(512)S(1)} %fusion.4, f32[8,24]{1,0:T(8,128)S(1)} %bitcast.145, pred[8,24]{1,0:T(8,128)(4,1)S(1)} %compare_bitcast_fusion), kind=kOutput, calls=%fused_computation.6 | convolution fusion | flops 454440960 | bytes 4156608 | tf_op jit(solution)/shard_map/bmt,bmp->tp/dot_general | solution.py:97
  (84 shorter events, 12.5 us)
Async XLA Ops:
  7.2 55.5 %copy-start = (bf16[288,4096]{1,0:T(8,128)(2,1)S(1)}, bf16[288,4096]{1,0:T(8,128)(2,1)}, u32[]{:S(2)}) copy-start(bf16[288,4096]{1,0:T(8,128)(2,1)} %param.6) | copy-start | bytes 7077892
  7.2 1.8 copy-start.1
  14.4 7.5 %copy-start.4 = (s32[32,4]{0,1:T(4,128)S(1)}, s32[32,4]{0,1:T(4,128)}, u32[]{:S(2)}) copy-start(s32[32,4]{0,1:T(4,128)} %param.7) | copy-start | bytes 1540
  14.4 44.5 %all-to-all-start.1 = ((bf16[8,24,4096]{2,1,0:T(8,128)(2,1)}), bf16[8,24,4096]{2,1,0:T(8,128)(2,1)}, u32[]{:S(2)}, u32[]{:S(2)}) async-start(bf16[8,24,4096]{2,1,0:T(8,128)(2,1)} %broadcast_select_fusion), calls=%async_computation.1 | async-start | bytes 3145728 | tf_op jit(solution)/shard_map/all_to_all | solution.py:46
  59.0 10.1 %all-to-all-start = ((bf16[8,1,24]{2,1,0:T(2,128)(2,1)}), bf16[8,1,24]{2,1,0:T(2,128)(2,1)S(1)}, u32[]{:S(2)}, u32[]{:S(2)}) async-start(bf16[8,1,24]{2,1,0:T(2,128)(2,1)} %reshape.404), calls=%async_computation | async-start | bytes 8192 | tf_op jit(solution)/shard_map/all_to_all | solution.py:47
  62.6 39.8 %copy-start.5 = (f32[288]{0:T(512)S(1)}, f32[288]{0:T(512)}, u32[]{:S(2)}) copy-start(f32[288]{0:T(512)} %param.9) | copy-start | bytes 3460
  62.6 37.6 %all-reduce.2.cloned.1.call-start = ((), (), s32[]{:S(2)}) async-start(), calls=%async_computation.4 | async-start | bytes 589824 | tf_op jit(solution)/shard_map/psum | solution.py:51
  66.0 57.1 %copy-start.6 = (f32[32]{0:T(128)S(1)}, f32[32]{0:T(128)}, u32[]{:S(2)}) copy-start(f32[32]{0:T(128)} %param.8) | copy-start | bytes 388
  100.2 53.5 %copy-start.2 = (f32[8,24,288]{2,1,0:T(8,128)S(1)}, f32[8,24,288]{2,1,0:T(8,128)}, u32[]{:S(2)}) copy-start(f32[8,24,288]{2,1,0:T(8,128)} %all-reduce.2.cloned.1.call-done) | copy-start | bytes 663556
  104.7 7.8 %collective-permute-start.6 = (f32[1,24]{1,0:T(1,128)S(1)}, f32[1,24]{1,0:T(1,128)S(1)}, u32[]{:S(2)}, u32[]{:S(2)}) collective-permute-start(f32[1,24]{1,0:T(1,128)S(1)} %get-tuple-element.10), channel_id=1, source_target_pairs={{0,28},{4,0},{8,4},{12,8},{16,12},{20,16},{24,20},{28,24},{1,29},{... | collective-permute-start | bytes 296 | tf_op jit(solution)/shard_map/ppermute | solution.py:75
  109.0 5.5 %collective-permute-start.5 = (f32[1,24]{1,0:T(1,128)S(1)}, f32[1,24]{1,0:T(1,128)S(1)}, u32[]{:S(2)}, u32[]{:S(2)}) collective-permute-start(f32[1,24]{1,0:T(1,128)S(1)} %get-tuple-element.11), channel_id=1, source_target_pairs={{0,24},{4,28},{8,0},{12,4},{16,8},{20,12},{24,16},{28,20},{1,25},{... | collective-permute-start | bytes 296 | tf_op jit(solution)/shard_map/ppermute | solution.py:75
  109.6 5.9 %collective-permute-start.4 = (f32[1,24]{1,0:T(1,128)S(1)}, f32[1,24]{1,0:T(1,128)S(1)}, u32[]{:S(2)}, u32[]{:S(2)}) collective-permute-start(f32[1,24]{1,0:T(1,128)S(1)} %get-tuple-element.12), channel_id=1, source_target_pairs={{0,20},{4,24},{8,28},{12,0},{16,4},{20,8},{24,12},{28,16},{1,21},{... | collective-permute-start | bytes 296 | tf_op jit(solution)/shard_map/ppermute | solution.py:75
  109.6 5.9 %collective-permute-start.3 = (f32[1,24]{1,0:T(1,128)S(1)}, f32[1,24]{1,0:T(1,128)S(1)}, u32[]{:S(2)}, u32[]{:S(2)}) collective-permute-start(f32[1,24]{1,0:T(1,128)S(1)} %get-tuple-element.13), channel_id=1, source_target_pairs={{0,16},{4,20},{8,24},{12,28},{16,0},{20,4},{24,8},{28,12},{1,17},{... | collective-permute-start | bytes 296 | tf_op jit(solution)/shard_map/ppermute | solution.py:75
  112.5 5.4 %collective-permute-start.2 = (f32[1,24]{1,0:T(1,128)S(1)}, f32[1,24]{1,0:T(1,128)S(1)}, u32[]{:S(2)}, u32[]{:S(2)}) collective-permute-start(f32[1,24]{1,0:T(1,128)S(1)} %get-tuple-element.14), channel_id=1, source_target_pairs={{0,12},{4,16},{8,20},{12,24},{16,28},{20,0},{24,4},{28,8},{1,13},{... | collective-permute-start | bytes 296 | tf_op jit(solution)/shard_map/ppermute | solution.py:75
  112.5 6.3 %collective-permute-start.1 = (f32[1,24]{1,0:T(1,128)S(1)}, f32[1,24]{1,0:T(1,128)S(1)}, u32[]{:S(2)}, u32[]{:S(2)}) collective-permute-start(f32[1,24]{1,0:T(1,128)S(1)} %get-tuple-element.15), channel_id=1, source_target_pairs={{0,8},{4,12},{8,16},{12,20},{16,24},{20,28},{24,0},{28,4},{1,9},{5... | collective-permute-start | bytes 296 | tf_op jit(solution)/shard_map/ppermute | solution.py:75
  114.5 6.3 %collective-permute-start = (f32[1,24]{1,0:T(1,128)S(1)}, f32[1,24]{1,0:T(1,128)S(1)}, u32[]{:S(2)}, u32[]{:S(2)}) collective-permute-start(f32[1,24]{1,0:T(1,128)S(1)} %get-tuple-element.16), channel_id=1, source_target_pairs={{0,4},{4,8},{8,12},{12,16},{16,20},{20,24},{24,28},{28,0},{1,5},{5... | collective-permute-start | bytes 296 | tf_op jit(solution)/shard_map/ppermute | solution.py:75
  154.4 6.5 %collective-permute-start.13 = (f32[1,24]{1,0:T(1,128)S(1)}, f32[1,24]{1,0:T(1,128)S(1)}, u32[]{:S(2)}, u32[]{:S(2)}) collective-permute-start(f32[1,24]{1,0:T(1,128)S(1)} %get-tuple-element.2), channel_id=1, source_target_pairs={{0,28},{4,0},{8,4},{12,8},{16,12},{20,16},{24,20},{28,24},{1,29},{... | collective-permute-start | bytes 296 | tf_op jit(solution)/shard_map/ppermute | solution.py:75
  155.0 7.3 %collective-permute-start.12 = (f32[1,24]{1,0:T(1,128)S(1)}, f32[1,24]{1,0:T(1,128)S(1)}, u32[]{:S(2)}, u32[]{:S(2)}) collective-permute-start(f32[1,24]{1,0:T(1,128)S(1)} %get-tuple-element.3), channel_id=1, source_target_pairs={{0,24},{4,28},{8,0},{12,4},{16,8},{20,12},{24,16},{28,20},{1,25},{... | collective-permute-start | bytes 296 | tf_op jit(solution)/shard_map/ppermute | solution.py:75
  156.4 6.4 %collective-permute-start.11 = (f32[1,24]{1,0:T(1,128)S(1)}, f32[1,24]{1,0:T(1,128)S(1)}, u32[]{:S(2)}, u32[]{:S(2)}) collective-permute-start(f32[1,24]{1,0:T(1,128)S(1)} %get-tuple-element.4), channel_id=1, source_target_pairs={{0,20},{4,24},{8,28},{12,0},{16,4},{20,8},{24,12},{28,16},{1,21},{... | collective-permute-start | bytes 296 | tf_op jit(solution)/shard_map/ppermute | solution.py:75
  157.9 5.0 %collective-permute-start.10 = (f32[1,24]{1,0:T(1,128)S(1)}, f32[1,24]{1,0:T(1,128)S(1)}, u32[]{:S(2)}, u32[]{:S(2)}) collective-permute-start(f32[1,24]{1,0:T(1,128)S(1)} %get-tuple-element.5), channel_id=1, source_target_pairs={{0,16},{4,20},{8,24},{12,28},{16,0},{20,4},{24,8},{28,12},{1,17},{... | collective-permute-start | bytes 296 | tf_op jit(solution)/shard_map/ppermute | solution.py:75
  159.4 5.4 %collective-permute-start.9 = (f32[1,24]{1,0:T(1,128)S(1)}, f32[1,24]{1,0:T(1,128)S(1)}, u32[]{:S(2)}, u32[]{:S(2)}) collective-permute-start(f32[1,24]{1,0:T(1,128)S(1)} %get-tuple-element.6), channel_id=1, source_target_pairs={{0,12},{4,16},{8,20},{12,24},{16,28},{20,0},{24,4},{28,8},{1,13},{... | collective-permute-start | bytes 296 | tf_op jit(solution)/shard_map/ppermute | solution.py:75
  160.8 5.4 %collective-permute-start.8 = (f32[1,24]{1,0:T(1,128)S(1)}, f32[1,24]{1,0:T(1,128)S(1)}, u32[]{:S(2)}, u32[]{:S(2)}) collective-permute-start(f32[1,24]{1,0:T(1,128)S(1)} %get-tuple-element.7), channel_id=1, source_target_pairs={{0,8},{4,12},{8,16},{12,20},{16,24},{20,28},{24,0},{28,4},{1,9},{5... | collective-permute-start | bytes 296 | tf_op jit(solution)/shard_map/ppermute | solution.py:75
  162.3 6.3 %collective-permute-start.7 = (f32[1,24]{1,0:T(1,128)S(1)}, f32[1,24]{1,0:T(1,128)S(1)}, u32[]{:S(2)}, u32[]{:S(2)}) collective-permute-start(f32[1,24]{1,0:T(1,128)S(1)} %get-tuple-element.8), channel_id=1, source_target_pairs={{0,4},{4,8},{8,12},{12,16},{16,20},{20,24},{24,28},{28,0},{1,5},{5... | collective-permute-start | bytes 296 | tf_op jit(solution)/shard_map/ppermute | solution.py:75
  170.9 34.5 %copy-start.3 = (f32[32]{0:T(128)}, f32[32]{0:T(128)S(1)}, u32[]{:S(2)}) copy-start(f32[32]{0:T(128)S(1)} %log_subtract_fusion.2) | copy-start | bytes 388
Sparse Core Ops, SparseCore 0:
  66.3 33.7 all-reduce.1
